TPU v7x, 32 devices: a whole 2x2x4 slice. The times are simulated.
32 devices in a mesh: gx: 2 (over x), gy: 4 (over z), gz: 4 (over y, core).
Axes of the slice: x: 2, y: 2, z: 4, core: 2. Of those that a mesh axis runs over, the one named last changes fastest.
Arguments:
- camera_tiles: bfloat16 [6, 256, 1024], P(None, ('gx', 'gy'), 'gz'), may hold values from 0.049804688 to 4
- slot_lines: int32 [6, 256], P(None, ('gx', 'gy')), may hold values from -1 to 127, as said below
- view_shifts: int32 [6], replicated, may hold values from -8 to 8, as said below
- psf_width: float32 [6], replicated, may hold values from 16 to 64
- background: float32 [6], replicated, may hold values from 0.1 to 1
Outputs:
- joined_volume: float32 [16, 64, 1024], P('gx', 'gy', 'gz')
- coarse_level: float32 [8, 32, 512], P('gx', ('gy', 'gz'))
Inputs may be any that keep to these rules, and one draw needn't show every extreme that they name: `slot_lines`: each entry is -1 (an empty slot) or a line of the owner brick, numbered x-major over its 8 x 16 columns. The 32 slots of one source block are 8 buckets of 4 slots in owner order, owners numbered with y fastest; the live slots of a bucket come first, and any bucket may hold 0 to 4 live slots. In every view some owner receives a full bucket from every source block. Lists are the same for all z layers. `view_shifts`: in every draw some view has shift 8 and another -8.
All inputs are finite; a program needn't handle non-finite values.
Results may differ from a plain program's by a relative error of at most 0.002.
Values may be sent and summed in bfloat16 or wider, within the bound.
A program may use at most 64 MiB of HBM per device.

v0:
```python
import functools

import jax
import jax.numpy as jnp
from jax import lax
from jax.experimental import pallas as pl
from jax.experimental.pallas import tpu as pltpu
from jax.sharding import PartitionSpec as P

PSF_REACH = 64
CX = 8
CY = 16
CAPACITY = 4
ROWS = 32
LIST_ROW = 24
LANES = 128
MESH = pl.DeviceIdType.MESH


def iota(shape, dim):
    return lax.broadcasted_iota(jnp.int32, shape, dim)


def dot(a, b):
    return jnp.dot(a, b, preferred_element_type=jnp.float32)


def dot_split(a, b):
    high = a.astype(jnp.bfloat16)
    low = (a - high.astype(jnp.float32)).astype(jnp.bfloat16)
    return dot(high, b) + dot(low, b)


def tap(distance):
    weight = jnp.where((distance == 1) | (distance == 2), 3.0, 1.0)
    return jnp.where((distance >= 0) & (distance <= 3), weight, 0.0)


def kernel(
    n_gx, n_gy, n_gz, shifts, widths, backs, tiles_in, lists_in, joined_out, coarse_out,
    tiles, lists, local_sem, thin, weights, members, send, got, halo, vd, est, est_b, ratio, blur_w, corr_w, parts, sums,
    send_sem, got_sem, pass_sem, halo_sem, part_sem, sum_sem,
):
    views, slots, depth = tiles_in.shape
    take = [
        pltpu.make_async_copy(tiles_in, tiles, local_sem.at[0]),
        pltpu.make_async_copy(lists_in, lists, local_sem.at[1]),
    ]
    for copy in take:
        copy.start()
    n = n_gx * n_gy
    blocks = depth // LANES
    lines = CX * CY
    rows_y = CY // 2 // n_gz
    rows_x = CX // 2
    gx, gy, gz = lax.axis_index("gx"), lax.axis_index("gy"), lax.axis_index("gz")
    me = gx * n_gy + gy
    group = n_gz + 2

    def owner(o):
        return (o // n_gy, o % n_gy, gz)

    def tile_copy(src, dst, target):
        return pltpu.make_async_remote_copy(
            src_ref=send.at[dst], dst_ref=got.at[src], send_sem=send_sem.at[dst],
            recv_sem=got_sem.at[src], device_id=target, device_id_type=MESH,
        )

    def halo_copy(buf, src, side, target):
        return pltpu.make_async_remote_copy(
            src_ref=buf.at[src, :LIST_ROW], dst_ref=halo.at[side, src, :LIST_ROW], send_sem=pass_sem.at[side, src],
            recv_sem=halo_sem.at[side, src], device_id=target, device_id_type=MESH,
        )

    def part_copy(p, c, src_z, target):
        return pltpu.make_async_remote_copy(
            src_ref=parts.at[p], dst_ref=sums.at[c, src_z], send_sem=part_sem.at[p],
            recv_sem=sum_sem.at[c, src_z], device_id=target, device_id_type=MESH,
        )

    def in_x(x):
        return (x >= 0) & (x < n_gx)

    def in_y(y):
        return (y >= 0) & (y < n_gy)

    def part_sends(act):
        for dxi, dx in enumerate((-1, 0, 1)):
            @pl.when(in_x(gx + dx))
            def _():
                for r in range(1 if dx == 0 else 0, n_gz):
                    k = (gz + r) % n_gz
                    act(dxi * group + k, dxi * 3 + 1, (gx + dx, gy, k))

                @pl.when(in_y(gy + 1))
                def _():
                    act(dxi * group + n_gz, dxi * 3 + 2, (gx + dx, gy + 1, 0))

                @pl.when(in_y(gy - 1))
                def _():
                    act(dxi * group + n_gz + 1, dxi * 3, (gx + dx, gy - 1, n_gz - 1))

    def part_sources(act):
        for dxi, dx in enumerate((-1, 0, 1)):
            @pl.when(in_x(gx - dx))
            def _():
                for r in range(1 if dx == 0 else 0, n_gz):
                    z = (gz + r) % n_gz
                    act(dxi * 3 + 1, z, (gx - dx, gy, z))

                @pl.when(in_y(gy - 1) & (gz == 0))
                def _():
                    for z in range(n_gz):
                        act(dxi * 3 + 2, z, (gx - dx, gy - 1, z))

                @pl.when(in_y(gy + 1) & (gz == n_gz - 1))
                def _():
                    for z in range(n_gz):
                        act(dxi * 3, z, (gx - dx, gy + 1, z))

    sums[...] = jnp.zeros_like(sums)
    rest = (2, n, ROWS - LIST_ROW, depth)
    halo[:, :, LIST_ROW:] = jnp.zeros(rest, jnp.bfloat16)

    barrier = pltpu.get_barrier_semaphore()

    def greet(target):
        pl.semaphore_signal(barrier, inc=1, device_id=target, device_id_type=MESH)

    def greet_owner(i, carry):
        greet(owner((me + n - i) % n))
        return carry

    lax.fori_loop(1, n, greet_owner, 0)

    @pl.when(gz > 0)
    def _():
        greet((gx, gy, gz - 1))

    @pl.when(gz < n_gz - 1)
    def _():
        greet((gx, gy, gz + 1))

    part_sources(lambda c, z, source: greet(source))

    used = slice(0, LIST_ROW)

    @pl.when(gz == 0)
    def _():
        halo[0, :, used] = jnp.zeros_like(halo[0, :, used])

    @pl.when(gz == n_gz - 1)
    def _():
        halo[1, :, used] = jnp.zeros_like(halo[1, :, used])

    for copy in take:
        copy.wait()
    flat = tiles[...].reshape(views * slots, depth)
    listed = (lists[...] + 1).astype(jnp.float32).astype(jnp.bfloat16)
    batch = min(n, 8)
    for first in range(0, n, batch):
        shape = (batch * ROWS, views * slots)
        row = iota(shape, 0)
        q = row & (ROWS - 1)
        o = first + row // ROWS
        wanted = (q // CAPACITY) * slots + o * CAPACITY + (q & (CAPACITY - 1))
        pick = (iota(shape, 1) == wanted) & (q < views * CAPACITY)
        packed = dot(pick.astype(jnp.float32).astype(jnp.bfloat16), flat)
        shape = (slots, batch * depth)
        lane = iota(shape, 1)
        spot = (first + lane // depth) * CAPACITY + (lane & (CAPACITY - 1))
        spread = dot(listed, (iota(shape, 0) == spot).astype(jnp.float32).astype(jnp.bfloat16))
        lane = iota(spread.shape, 1) & (depth - 1)
        mine = (lane // CAPACITY) == (me % 8) * (ROWS // CAPACITY) + iota(spread.shape, 0)
        ids = jnp.sum(jnp.where(mine, spread, 0.0), axis=0, keepdims=True)
        list_row = iota((ROWS, depth), 0) == LIST_ROW + me // 8
        for i in range(batch):
            body = packed[i * ROWS : (i + 1) * ROWS]
            body = body + jnp.where(list_row, ids[:, i * depth : (i + 1) * depth], 0.0)
            send[first + i] = body.astype(jnp.bfloat16)
    got[me] = send[me]

    step = (iota((LANES, LANES), 1) - iota((LANES, LANES), 0)).astype(jnp.float32)
    reach = iota((1, LANES), 1)
    for v in range(views):
        shift = shifts[v].astype(jnp.float32)
        inv = 1.0 / jnp.full((1, LANES), widths[v], jnp.float32)
        curve = -0.5 * inv * inv
        far = reach.astype(jnp.float32)
        half = jnp.where((reach >= 1) & (reach <= PSF_REACH), jnp.exp(far * far * curve), 0.0)
        scale = 1.0 / (1.0 + 2.0 * jnp.sum(half, axis=1, keepdims=True))
        for m in range(3):
            for sign, table in ((-1.0, blur_w), (1.0, corr_w)):
                off = step - (m - 1.0) * LANES + sign * shift
                value = jnp.exp(off * off * curve) * scale
                value = jnp.where(jnp.abs(off) <= PSF_REACH, value, 0.0).astype(jnp.bfloat16)
                if table is blur_w:
                    table[m * LANES : (m + 1) * LANES, v * LANES : (v + 1) * LANES] = value
                else:
                    at = (m * views + v) * LANES
                    table[at : at + LANES, :] = value

    half_depth = depth // 2
    z = iota(((blocks + 2) * LANES, half_depth), 0)
    k = iota(((blocks + 2) * LANES, half_depth), 1)
    thin[...] = tap(z - LANES - 2 * k + 1).astype(jnp.bfloat16)
    r = iota((8, lines), 0)
    column = iota((8, lines), 1)
    rows = []
    for dx in (-1, 0, 1):
        for t in range(group):
            dy, z_part = (0, t) if t < n_gz else ((1, 0) if t == n_gz else (-1, n_gz - 1))
            i = rows_x * dx + r // rows_y
            j = (CY // 2) * dy + rows_y * z_part + r % rows_y
            weight = tap(column // CY - 2 * i + 1) * tap(column % CY - 2 * j + 1)
            rows.append(jnp.where(r < rows_x * rows_y, weight, 0.0))
    weights[...] = jnp.concatenate(rows, axis=0).astype(jnp.bfloat16)

    count = n - 1
    count = count + jnp.where(gz > 0, 1, 0) + jnp.where(gz < n_gz - 1, 1, 0)
    for dx in (-1, 0, 1):
        per = n_gz - (1 if dx == 0 else 0)
        per = per + jnp.where(in_y(gy + 1), 1, 0) + jnp.where(in_y(gy - 1), 1, 0)
        count = count + jnp.where(in_x(gx + dx), per, 0)
    pl.semaphore_wait(barrier, count)

    def send_tile(i, carry):
        o = (me + i) % n
        tile_copy(me, o, owner(o)).start()
        return carry

    lax.fori_loop(1, n, send_tile, 0)

    def pass_on(buf, src):
        @pl.when(gz > 0)
        def _():
            halo_copy(buf, src, 1, (gx, gy, gz - 1)).start()

        @pl.when(gz < n_gz - 1)
        def _():
            halo_copy(buf, src, 0, (gx, gy, gz + 1)).start()

    pass_on(send, me)

    def take_tile(i, carry):
        src = (me + n - i) % n
        tile_copy(src, me, owner(src)).wait_recv()
        pass_on(got, src)
        return carry

    lax.fori_loop(1, n, take_tile, 0)

    ids = got[0, 16:32].astype(jnp.float32)
    for src in range(1, n):
        ids = ids + got[src, 16:32].astype(jnp.float32)
    line = (iota((lines, batch * ROWS), 0) + 1).astype(jnp.float32)
    lane = iota((lines, batch * ROWS), 1)
    view = (lane // CAPACITY) & (ROWS // CAPACITY - 1)

    for first in range(0, n, batch):
        at = LIST_ROW - 16 + first // 8
        hit = ids[at : at + 1, : batch * ROWS] == line
        for v in range(views):
            owned = jnp.where(hit & (view == v), 1.0, 0.0)
            members[first // batch, v * lines : (v + 1) * lines] = owned.astype(jnp.bfloat16)
        owned = jnp.where(hit & (view < views), 1.0, 0.0)
        members[first // batch, views * lines :] = owned.astype(jnp.bfloat16)

    def landed(rows, load):
        total = None
        for first in range(0, n, batch):
            term = dot(members[first // batch, rows], load(first))
            total = term if total is None else total + term
        return total

    every = slice(0, views * lines)
    merged = slice(views * lines, (views + 1) * lines)

    def own(first):
        return got[first : first + batch].reshape(batch * ROWS, depth)

    def beside(side, lanes):
        return lambda first: halo[side, first : first + batch, :, lanes].reshape(batch * ROWS, -1)

    whole = slice(0, depth)
    middle = landed(merged, own) / views
    est[:, LANES : LANES + depth] = middle
    est_b[:, depth : 2 * depth] = middle.astype(jnp.bfloat16)

    def keep(b, value):
        for v in range(views):
            vd[b, :, v * LANES : (v + 1) * LANES] = value[v * lines : (v + 1) * lines]

    value = landed(every, own)
    for b in range(blocks):
        keep(b + 1, value[:, b * LANES : (b + 1) * LANES])

    @pl.when(gz > 0)
    def _():
        for src in range(n):
            halo_copy(got, src, 0, (gx, gy, gz)).wait_recv()

    @pl.when(gz < n_gz - 1)
    def _():
        for src in range(n):
            halo_copy(got, src, 1, (gx, gy, gz)).wait_recv()

    left = landed(merged, beside(0, whole)) / views
    right = landed(merged, beside(1, whole)) / views
    est[:, :LANES] = left[:, depth - LANES :]
    est[:, LANES + depth :] = right[:, :LANES]
    est_b[:, :depth] = left.astype(jnp.bfloat16)
    est_b[:, 2 * depth :] = right.astype(jnp.bfloat16)
    keep(0, landed(every, beside(0, slice(depth - LANES, depth))))
    keep(blocks + 1, landed(every, beside(1, slice(0, LANES))))

    back = jnp.concatenate([jnp.full((1, LANES), backs[v], jnp.float32) for v in range(views)], axis=1)
    start = depth // LANES - 2
    for b in range(blocks + 2):
        blurred = dot(est_b[:, (start + b) * LANES : (start + b + 3) * LANES], blur_w[...])
        ratio[:, b * views * LANES : (b + 1) * views * LANES] = (
            vd[b] / (blurred + back)
        ).astype(jnp.bfloat16)
    joined = []
    span = views * LANES
    for b in range(blocks + 2):
        low, high = max(b - 1, 0), min(b + 2, blocks + 2)
        correction = dot(
            ratio[:, low * span : high * span],
            corr_w[(low - b + 1) * span : (high - b + 1) * span, :],
        )
        joined.append(est[:, b * LANES : (b + 1) * LANES] * (correction / views))
    for b in range(blocks):
        joined_out[:, :, b * LANES : (b + 1) * LANES] = joined[b + 1].reshape(CX, CY, LANES)

    halved = dot_split(jnp.concatenate(joined, axis=1), thin[...]) * (1.0 / 8)
    high = halved.astype(jnp.bfloat16)
    low = (halved - high.astype(jnp.float32)).astype(jnp.bfloat16)
    shares = (dot(weights[...], high) + dot(weights[...], low)) * (1.0 / 64)
    parts[...] = shares.reshape(3 * group, 8, half_depth)
    part_sends(lambda p, c, target: part_copy(p, c, gz, target).start())
    sums[4, gz] = parts[group + gz]

    def sent_tile(i, carry):
        o = (me + i) % n
        tile_copy(me, o, owner(o)).wait_send()
        return carry

    lax.fori_loop(1, n, sent_tile, 0)

    @pl.when(gz > 0)
    def _():
        for src in range(n):
            halo_copy(got, src, 1, (gx, gy, gz)).wait_send()

    @pl.when(gz < n_gz - 1)
    def _():
        for src in range(n):
            halo_copy(got, src, 0, (gx, gy, gz)).wait_send()

    part_sources(lambda c, s, source: part_copy(0, c, s, source).wait_recv())
    for s in range(n_gz):
        total = sums[0, s]
        for c in range(1, 9):
            total = total + sums[c, s]
        for i in range(rows_x):
            coarse_out[i, :, s * half_depth : (s + 1) * half_depth] = total[i * rows_y : (i + 1) * rows_y]
    part_sends(lambda p, c, target: part_copy(p, c, gz, target).wait_send())


def hand_on(joined, coarse, joined_out, coarse_out, sem):
    pairs = ((joined, joined_out), (coarse, coarse_out))
    put = [pltpu.make_async_copy(a, b, sem.at[i]) for i, (a, b) in enumerate(pairs)]
    for copy in put:
        copy.start()
    for copy in put:
        copy.wait()


def on_device(n_gx, n_gy, n_gz, camera_tiles, slot_lines, view_shifts, psf_width, background):
    views, slots, depth = camera_tiles.shape
    n = n_gx * n_gy
    packets = 3 * (n_gz + 2)
    width = depth + 2 * LANES
    smem = pl.BlockSpec(memory_space=pltpu.SMEM)
    vmem = pl.BlockSpec(memory_space=pltpu.VMEM)
    hbm = pl.BlockSpec(memory_space=pl.ANY)
    results = pl.pallas_call(
        functools.partial(kernel, n_gx, n_gy, n_gz),
        out_shape=(
            pltpu.VMEM((CX, CY, depth), jnp.float32),
            pltpu.VMEM((CX // 2, CY // 2 // n_gz, depth // 2 * n_gz), jnp.float32),
        ),
        in_specs=[smem, smem, smem, hbm, hbm],
        out_specs=(vmem, vmem),
        scratch_shapes=[
            pltpu.VMEM((views, slots, depth), jnp.bfloat16),
            pltpu.VMEM((views, slots), jnp.int32),
            pltpu.SemaphoreType.DMA((2,)),
            pltpu.VMEM((width, depth // 2), jnp.bfloat16),
            pltpu.VMEM((packets * 8, CX * CY), jnp.bfloat16),
            pltpu.VMEM((-(-n // 8), (views + 1) * CX * CY, min(n, 8) * ROWS), jnp.bfloat16),
            pltpu.VMEM((n, ROWS, depth), jnp.bfloat16),
            pltpu.VMEM((n, ROWS, depth), jnp.bfloat16),
            pltpu.VMEM((2, n, ROWS, depth), jnp.bfloat16),
            pltpu.VMEM((depth // LANES + 2, CX * CY, views * LANES), jnp.float32),
            pltpu.VMEM((CX * CY, width), jnp.float32),
            pltpu.VMEM((CX * CY, 3 * depth), jnp.bfloat16),
            pltpu.VMEM((CX * CY, width * views), jnp.bfloat16),
            pltpu.VMEM((3 * LANES, views * LANES), jnp.bfloat16),
            pltpu.VMEM((3 * views * LANES, LANES), jnp.bfloat16),
            pltpu.VMEM((packets, 8, depth // 2), jnp.float32),
            pltpu.VMEM((9, n_gz, 8, depth // 2), jnp.float32),
            pltpu.SemaphoreType.DMA((n,)),
            pltpu.SemaphoreType.DMA((n,)),
            pltpu.SemaphoreType.DMA((2, n)),
            pltpu.SemaphoreType.DMA((2, n)),
            pltpu.SemaphoreType.DMA((packets,)),
            pltpu.SemaphoreType.DMA((9, n_gz)),
        ],
        compiler_params=pltpu.CompilerParams(collective_id=0, has_side_effects=True),
    )(view_shifts, psf_width, background, camera_tiles, slot_lines)
    return pl.pallas_call(
        hand_on,
        out_shape=tuple(jax.ShapeDtypeStruct(r.shape, r.dtype) for r in results),
        in_specs=[vmem, vmem],
        out_specs=(hbm, hbm),
        scratch_shapes=[pltpu.SemaphoreType.DMA((2,))],
        compiler_params=pltpu.CompilerParams(has_side_effects=True),
    )(*[pltpu.with_memory_space_constraint(r, pltpu.VMEM) for r in results])


def solution(mesh):
    sizes = (mesh.shape["gx"], mesh.shape["gy"], mesh.shape["gz"])
    in_specs = (P(None, ("gx", "gy"), "gz"), P(None, ("gx", "gy")), P(), P(), P())
    out_specs = (P("gx", "gy", "gz"), P("gx", ("gy", "gz"), None))
    return jax.shard_map(
        functools.partial(on_device, *sizes), mesh=mesh, in_specs=in_specs, out_specs=out_specs,
        check_vma=False,
    )
```

profile of v0, /device:TPU:0, one launch (start us, length us, event | category | flops | bytes accessed | tf_op | source)
XLA Modules:
  0.0 20.4 jit_solution(4919179515617305084)
XLA Ops:
  0.6 19.1 %shard_map.68 = (f32[8,16,256]{2,1,0:T(8,128)S(1)}, f32[4,2,512]{2,1,0:T(2,128)S(1)}) custom-call(s32[6]{0:T(128)} %shifts.1, f32[6]{0:T(128)} %widths.1, f32[6]{0:T(128)} %backs.1, bf16[6,32,256]{2,1,0:T(8,128)(2,1)} %tiles_in.1, s32[6,32]{1,0:T(8,128)} %lists_in.1), custom_call_target="tpu_custom_call" | custom-call | tf_op jit(solution)/shard_map/pallas_call | solution.py:388
  19.7 0.7 %shard_map.69 = (f32[8,16,256]{2,1,0:T(8,128)}, f32[4,2,512]{2,1,0:T(2,128)}) custom-call(f32[8,16,256]{2,1,0:T(8,128)S(1)} %get-tuple-element.4.joined, f32[4,2,512]{2,1,0:T(2,128)S(1)} %get-tuple-element.5.coarse), custom_call_target="tpu_custom_call" | custom-call | tf_op jit(solution)/shard_map/pallas_call | solution.py:423
where the time goes:
time: 20.5 us; the launch traced here: 20.4 us
  Pallas kernels  19.7 us (96%)
  between operations  0.64 us (3%)
    pallas_call x1, Pallas kernels, on_device(): pl.pallas_call(functools.partial(kernel, n_gx, n_gy, n_gz), out_shape=(pl...  19.1 us
    pallas_call x1, Pallas kernels, on_device(): pl.pallas_call(hand_on, out_shape=tuple((jax.ShapeDtypeStruct(r.shape, r....  0.68 us

commit v1 on v0

v1 whole, which is shorter than its diff:
```python
import functools

import jax
import jax.numpy as jnp
from jax import lax
from jax.experimental import pallas as pl
from jax.experimental.pallas import tpu as pltpu
from jax.sharding import PartitionSpec as P

PSF_REACH = 64
CX = 8
CY = 16
CAPACITY = 4
ROWS = 32
LIST_ROW = 24
LANES = 128
MESH = pl.DeviceIdType.MESH


def iota(shape, dim):
    return lax.broadcasted_iota(jnp.int32, shape, dim)


def dot(a, b):
    return jnp.dot(a, b, preferred_element_type=jnp.float32)


def dot_split(a, b):
    high = a.astype(jnp.bfloat16)
    low = (a - high.astype(jnp.float32)).astype(jnp.bfloat16)
    return dot(high, b) + dot(low, b)


def tap(distance):
    weight = jnp.where((distance == 1) | (distance == 2), 3.0, 1.0)
    return jnp.where((distance >= 0) & (distance <= 3), weight, 0.0)


def spread_lanes(block, width):
    return jnp.concatenate([block] * (width // LANES), axis=1) if width > LANES else block


def kernel(
    n_gx, n_gy, n_gz, shifts_in, widths_in, backs_in, tiles_in, lists_in, joined_out, coarse_out,
    shifts, widths, backs, tiles, lists, local_sem, thin, weights, members, send, got, halo, vd, vd_side, est_b, partial,
    ratio, blur_w, corr_w, parts, sums, send_sem, got_sem, pass_sem, halo_sem, part_sem, sum_sem,
):
    views, slots, depth = tiles_in.shape
    n = n_gx * n_gy
    blocks = depth // LANES
    lines = CX * CY
    rows_y = CY // 2 // n_gz
    rows_x = CX // 2
    gx, gy, gz = lax.axis_index("gx"), lax.axis_index("gy"), lax.axis_index("gz")
    me = gx * n_gy + gy
    group = n_gz + 2
    used = blocks * ROWS - (ROWS - LIST_ROW if n <= 32 else 0)
    last = (blocks - 1) * ROWS

    def owner(o):
        return (o // n_gy, o % n_gy, gz)

    def tile_copy(src, dst, target):
        return pltpu.make_async_remote_copy(
            src_ref=send.at[dst, :used], dst_ref=got.at[src, :used], send_sem=send_sem.at[dst],
            recv_sem=got_sem.at[src], device_id=target, device_id_type=MESH,
        )

    def halo_copy(buf, src, side, target):
        first = last if side == 0 else 0
        return pltpu.make_async_remote_copy(
            src_ref=buf.at[src, first : first + LIST_ROW], dst_ref=halo.at[side, src, :LIST_ROW],
            send_sem=pass_sem.at[side, src], recv_sem=halo_sem.at[side, src], device_id=target, device_id_type=MESH,
        )

    def part_copy(p, c, src_z, target):
        return pltpu.make_async_remote_copy(
            src_ref=parts.at[p], dst_ref=sums.at[c, src_z], send_sem=part_sem.at[p],
            recv_sem=sum_sem.at[c, src_z], device_id=target, device_id_type=MESH,
        )

    def in_x(x):
        return (x >= 0) & (x < n_gx)

    def in_y(y):
        return (y >= 0) & (y < n_gy)

    def part_sends(act):
        for dxi, dx in ((0, -1), (2, 1), (1, 0)):
            @pl.when(in_x(gx + dx))
            def _():
                @pl.when(in_y(gy + 1))
                def _():
                    act(dxi * group + n_gz, dxi * 3 + 2, (gx + dx, gy + 1, 0))

                @pl.when(in_y(gy - 1))
                def _():
                    act(dxi * group + n_gz + 1, dxi * 3, (gx + dx, gy - 1, n_gz - 1))

                for r in range(1 if dx == 0 else 0, n_gz):
                    k = (gz + r) % n_gz
                    act(dxi * group + k, dxi * 3 + 1, (gx + dx, gy, k))

    def part_sources(act):
        for dxi, dx in enumerate((-1, 0, 1)):
            @pl.when(in_x(gx - dx))
            def _():
                for r in range(1 if dx == 0 else 0, n_gz):
                    z = (gz + r) % n_gz
                    act(dxi * 3 + 1, z, (gx - dx, gy, z))

                @pl.when(in_y(gy - 1) & (gz == 0))
                def _():
                    for z in range(n_gz):
                        act(dxi * 3 + 2, z, (gx - dx, gy - 1, z))

                @pl.when(in_y(gy + 1) & (gz == n_gz - 1))
                def _():
                    for z in range(n_gz):
                        act(dxi * 3, z, (gx - dx, gy + 1, z))

    barrier = pltpu.get_barrier_semaphore()

    def greet(target):
        pl.semaphore_signal(barrier, inc=1, device_id=target, device_id_type=MESH)

    def greet_owner(i, carry):
        greet(owner((me + n - i) % n))
        return carry

    lax.fori_loop(1, n, greet_owner, 0)

    @pl.when(gz > 0)
    def _():
        greet((gx, gy, gz - 1))

    @pl.when(gz < n_gz - 1)
    def _():
        greet((gx, gy, gz + 1))

    part_sources(lambda c, z, source: greet(source))

    pairs = (
        (tiles_in, tiles), (lists_in, lists), (shifts_in, shifts), (widths_in, widths), (backs_in, backs),
    )
    take = [pltpu.make_async_copy(a, b, local_sem.at[i]) for i, (a, b) in enumerate(pairs)]
    for copy in take:
        copy.start()

    halo[:, :, LIST_ROW:] = jnp.zeros((2, n, ROWS - LIST_ROW, LANES), jnp.bfloat16)
    if used < blocks * ROWS:
        got[:, used:] = jnp.zeros((n, blocks * ROWS - used, LANES), jnp.bfloat16)

    @pl.when(gz == 0)
    def _():
        halo[0, :, :LIST_ROW] = jnp.zeros((n, LIST_ROW, LANES), jnp.bfloat16)

    @pl.when(gz == n_gz - 1)
    def _():
        halo[1, :, :LIST_ROW] = jnp.zeros((n, LIST_ROW, LANES), jnp.bfloat16)

    for copy in take:
        copy.wait()
    flat = tiles[...].reshape(views * slots, depth)
    listed = (lists[...] + 1).astype(jnp.float32).astype(jnp.bfloat16)
    batch = min(n, 8)
    list_block, list_row = me // 32, LIST_ROW + me // 4 % 8
    for first in range(0, n, batch):
        shape = (batch * ROWS, views * slots)
        row = iota(shape, 0)
        q = row & (ROWS - 1)
        o = first + row // ROWS
        wanted = (q // CAPACITY) * slots + o * CAPACITY + (q & (CAPACITY - 1))
        pick = (iota(shape, 1) == wanted) & (q < views * CAPACITY)
        packed = dot(pick.astype(jnp.float32).astype(jnp.bfloat16), flat)
        shape = (slots, batch * LANES)
        lane = iota(shape, 1)
        spot = (first + lane // LANES) * CAPACITY + (lane & (CAPACITY - 1))
        spread = dot(listed, (iota(shape, 0) == spot).astype(jnp.float32).astype(jnp.bfloat16))
        lane = iota(spread.shape, 1) & (LANES - 1)
        mine = (lane // CAPACITY) == (me % 4) * (ROWS // CAPACITY) + iota(spread.shape, 0)
        ids = jnp.sum(jnp.where(mine, spread, 0.0), axis=0, keepdims=True)
        for i in range(batch):
            for b in range(blocks):
                body = packed[i * ROWS : (i + 1) * ROWS, b * LANES : (b + 1) * LANES]
                listing = (iota(body.shape, 0) == list_row) & (list_block == b)
                body = body + jnp.where(listing, ids[:, i * LANES : (i + 1) * LANES], 0.0)
                send[first + i, b * ROWS : (b + 1) * ROWS] = body.astype(jnp.bfloat16)
    got[me, :used] = send[me, :used]

    step = (iota((LANES, LANES), 1) - iota((LANES, LANES), 0)).astype(jnp.float32)
    reach = iota((1, LANES), 1)
    span = views * LANES
    for b in range(blocks + 2):
        for d in range(blocks):
            if not 0 <= b - d <= 2:
                corr_w[b * span : (b + 1) * span, d * LANES : (d + 1) * LANES] = jnp.zeros((span, LANES), jnp.bfloat16)
    for v in range(views):
        shift = shifts[v].astype(jnp.float32)
        inv = 1.0 / jnp.full((1, LANES), widths[v], jnp.float32)
        curve = -0.5 * inv * inv
        far = reach.astype(jnp.float32)
        half = jnp.where((reach >= 1) & (reach <= PSF_REACH), jnp.exp(far * far * curve), 0.0)
        scale = 1.0 / (1.0 + 2.0 * jnp.sum(half, axis=1, keepdims=True))
        for m in range(3):
            for sign in (-1.0, 1.0):
                off = step - (m - 1.0) * LANES + sign * shift
                value = jnp.exp(off * off * curve) * scale
                value = jnp.where(jnp.abs(off) <= PSF_REACH, value, 0.0).astype(jnp.bfloat16)
                if sign < 0:
                    blur_w[m * LANES : (m + 1) * LANES, v * LANES : (v + 1) * LANES] = value
                    continue
                for d in range(blocks):
                    at = (d + m) * span + v * LANES
                    corr_w[at : at + LANES, d * LANES : (d + 1) * LANES] = value

    half_depth = depth // 2
    z = iota((depth, half_depth + LANES), 0)
    k = iota((depth, half_depth + LANES), 1)
    k = jnp.where(k == half_depth + LANES - 1, -1, k)
    thin[...] = tap(z - 2 * k + 1).astype(jnp.bfloat16)
    r = iota((8, lines), 0)
    column = iota((8, lines), 1)
    rows = []
    for dx in (-1, 0, 1):
        for t in range(group):
            dy, z_part = (0, t) if t < n_gz else ((1, 0) if t == n_gz else (-1, n_gz - 1))
            i = rows_x * dx + r // rows_y
            j = (CY // 2) * dy + rows_y * z_part + r % rows_y
            weight = tap(column // CY - 2 * i + 1) * tap(column % CY - 2 * j + 1)
            rows.append(jnp.where(r < rows_x * rows_y, weight, 0.0))
    weights[...] = jnp.concatenate(rows, axis=0).astype(jnp.bfloat16)

    count = n - 1
    count = count + jnp.where(gz > 0, 1, 0) + jnp.where(gz < n_gz - 1, 1, 0)
    for dx in (-1, 0, 1):
        per = n_gz - (1 if dx == 0 else 0)
        per = per + jnp.where(in_y(gy + 1), 1, 0) + jnp.where(in_y(gy - 1), 1, 0)
        count = count + jnp.where(in_x(gx + dx), per, 0)
    pl.semaphore_wait(barrier, count)

    def send_tile(i, carry):
        o = (me + i) % n
        tile_copy(me, o, owner(o)).start()
        return carry

    lax.fori_loop(1, n, send_tile, 0)

    def pass_on(buf, src):
        @pl.when(gz > 0)
        def _():
            halo_copy(buf, src, 1, (gx, gy, gz - 1)).start()

        @pl.when(gz < n_gz - 1)
        def _():
            halo_copy(buf, src, 0, (gx, gy, gz + 1)).start()

    pass_on(send, me)

    def take_tile(i, carry):
        src = (me + n - i) % n
        tile_copy(src, me, owner(src)).wait_recv()
        pass_on(got, src)
        return carry

    lax.fori_loop(1, n, take_tile, 0)

    total = None
    for b in range(blocks if used == blocks * ROWS else 1):
        at = b * ROWS + 16
        ids = got[0, at : at + 16].astype(jnp.float32)
        for src in range(1, n):
            ids = ids + got[src, at : at + 16].astype(jnp.float32)
        total = ids[8:] if total is None else jnp.concatenate([total, ids[8:]], axis=0)
    ids = total
    line = (iota((lines, batch * ROWS), 0) + 1).astype(jnp.float32)
    lane = iota((lines, batch * ROWS), 1)
    view = (lane // CAPACITY) & (ROWS // CAPACITY - 1)

    for first in range(0, n, batch):
        at = first // 4
        pieces = [ids[at + i : at + i + 1] for i in range(-(-batch // 4))]
        hit = jnp.concatenate(pieces, axis=1)[:, : batch * ROWS] == line
        for v in range(views):
            owned = jnp.where(hit & (view == v), 1.0, 0.0)
            members[first // batch, v * lines : (v + 1) * lines] = owned.astype(jnp.bfloat16)
        owned = jnp.where(hit & (view < views), 1.0, 0.0)
        members[first // batch, views * lines :] = owned.astype(jnp.bfloat16)

    def landed(rows, load):
        total = None
        for first in range(0, n, batch):
            term = dot(members[first // batch, rows], load(first))
            total = term if total is None else total + term
        return total

    every = slice(0, views * lines)
    merged = slice(views * lines, (views + 1) * lines)

    def own(first):
        return jnp.concatenate(
            [
                got[first : first + batch, b * ROWS : (b + 1) * ROWS].reshape(batch * ROWS, LANES)
                for b in range(blocks)
            ],
            axis=1,
        )

    def beside(first):
        return jnp.concatenate(
            [halo[side, first : first + batch].reshape(batch * ROWS, LANES) for side in range(2)], axis=1
        )

    est = landed(merged, own) / views
    est_b[...] = est.astype(jnp.bfloat16)
    vd[...] = landed(every, own)
    for b in range(blocks + 2):
        low, high = max(b - 1, 1), min(b + 2, blocks + 1)
        partial[:, b * span : (b + 1) * span] = dot(
            est_b[:, (low - 1) * LANES : (high - 1) * LANES],
            blur_w[(low - b + 1) * LANES : (high - b + 1) * LANES],
        )

    def ratio_of(b, blurred):
        for v in range(views):
            rows = slice(v * lines, (v + 1) * lines)
            if b == 0:
                data = vd_side[rows, :LANES]
            elif b == blocks + 1:
                data = vd_side[rows, LANES:]
            else:
                data = vd[rows, (b - 1) * LANES : b * LANES]
            value = data / (blurred[:, v * LANES : (v + 1) * LANES] + jnp.full((1, LANES), backs[v], jnp.float32))
            ratio[:, b * span + v * LANES : b * span + (v + 1) * LANES] = value.astype(jnp.bfloat16)

    for b in range(2, blocks):
        ratio_of(b, partial[:, b * span : (b + 1) * span])

    @pl.when(gz > 0)
    def _():
        for src in range(n):
            halo_copy(got, src, 0, (gx, gy, gz)).wait_recv()

    @pl.when(gz < n_gz - 1)
    def _():
        for src in range(n):
            halo_copy(got, src, 1, (gx, gy, gz)).wait_recv()

    side = (landed(merged, beside) / views).astype(jnp.bfloat16)
    vd_side[...] = landed(every, beside)
    for edge, near, m, column_block in ((0, 1, 0, 0), (blocks + 1, blocks, 2, 1)):
        here = side[:, column_block * LANES : (column_block + 1) * LANES]
        for b, w in ((edge, 1), (near, m)):
            blurred = partial[:, b * span : (b + 1) * span] + dot(here, blur_w[w * LANES : (w + 1) * LANES])
            if blocks == 1 and b == 1:
                partial[:, span : 2 * span] = blurred
            ratio_of(b, blurred)
    correction = dot(ratio[...], corr_w[...])
    joined = est * (correction / views)
    joined_out[...] = joined.reshape(CX, CY, depth)

    halved = dot_split(joined, thin[...]) * (1.0 / 8)
    high = halved.astype(jnp.bfloat16)
    low = (halved - high.astype(jnp.float32)).astype(jnp.bfloat16)
    shares = (dot(weights[...], high) + dot(weights[...], low)) * (1.0 / 64)
    parts[...] = shares.reshape(3 * group, 8, half_depth + LANES)
    part_sends(lambda p, c, target: part_copy(p, c, gz, target).start())
    sums[4, gz] = parts[group + gz]
    def sent_tile(i, carry):
        o = (me + i) % n
        tile_copy(me, o, owner(o)).wait_send()
        return carry

    lax.fori_loop(1, n, sent_tile, 0)

    @pl.when(gz > 0)
    def _():
        for src in range(n):
            halo_copy(got, src, 1, (gx, gy, gz)).wait_send()

    @pl.when(gz < n_gz - 1)
    def _():
        for src in range(n):
            halo_copy(got, src, 0, (gx, gy, gz)).wait_send()

    part_sources(lambda c, s, source: part_copy(0, c, s, source).wait_recv())
    totals = []
    for s in range(n_gz):
        total = sums[4, s]
        for dxi, dx in enumerate((-1, 0, 1)):
            for c, there in ((0, in_y(gy + 1) & (gz == n_gz - 1)), (1, gz >= 0), (2, in_y(gy - 1) & (gz == 0))):
                if dx == 0 and c == 1:
                    continue
                total = total + jnp.where(in_x(gx - dx) & there, sums[dxi * 3 + c, s], 0.0)
        totals.append(total)
    lane = iota((8, half_depth), 1)
    for s in range(n_gz):
        total = totals[s][:, :half_depth]
        if s > 0:
            after = totals[s - 1][:, half_depth : half_depth + LANES]
            total = total + jnp.where(lane == 0, spread_lanes(after, half_depth), 0.0)
        if s < n_gz - 1:
            before = totals[s + 1][:, half_depth : half_depth + LANES]
            total = total + jnp.where(lane == half_depth - 1, spread_lanes(before, half_depth), 0.0)
        for i in range(rows_x):
            coarse_out[i, :, s * half_depth : (s + 1) * half_depth] = total[i * rows_y : (i + 1) * rows_y]
    part_sends(lambda p, c, target: part_copy(p, c, gz, target).wait_send())


def hand_on(joined, coarse, joined_out, coarse_out, sem):
    pairs = ((joined, joined_out), (coarse, coarse_out))
    put = [pltpu.make_async_copy(a, b, sem.at[i]) for i, (a, b) in enumerate(pairs)]
    for copy in put:
        copy.start()
    for copy in put:
        copy.wait()


def on_device(n_gx, n_gy, n_gz, camera_tiles, slot_lines, view_shifts, psf_width, background):
    views, slots, depth = camera_tiles.shape
    n = n_gx * n_gy
    packets = 3 * (n_gz + 2)
    blocks = depth // LANES
    lines = CX * CY
    span = views * LANES
    vmem = pl.BlockSpec(memory_space=pltpu.VMEM)
    hbm = pl.BlockSpec(memory_space=pl.ANY)
    results = pl.pallas_call(
        functools.partial(kernel, n_gx, n_gy, n_gz),
        out_shape=(
            pltpu.VMEM((CX, CY, depth), jnp.float32),
            pltpu.VMEM((CX // 2, CY // 2 // n_gz, depth // 2 * n_gz), jnp.float32),
        ),
        in_specs=[hbm] * 5,
        out_specs=(vmem, vmem),
        scratch_shapes=[
            pltpu.SMEM((views,), jnp.int32),
            pltpu.SMEM((views,), jnp.float32),
            pltpu.SMEM((views,), jnp.float32),
            pltpu.VMEM((views, slots, depth), jnp.bfloat16),
            pltpu.VMEM((views, slots), jnp.int32),
            pltpu.SemaphoreType.DMA((5,)),
            pltpu.VMEM((depth, depth // 2 + LANES), jnp.bfloat16),
            pltpu.VMEM((packets * 8, lines), jnp.bfloat16),
            pltpu.VMEM((-(-n // 8), (views + 1) * lines, min(n, 8) * ROWS), jnp.bfloat16),
            pltpu.VMEM((n, blocks * ROWS, LANES), jnp.bfloat16),
            pltpu.VMEM((n, blocks * ROWS, LANES), jnp.bfloat16),
            pltpu.VMEM((2, n, ROWS, LANES), jnp.bfloat16),
            pltpu.VMEM((views * lines, depth), jnp.float32),
            pltpu.VMEM((views * lines, 2 * LANES), jnp.float32),
            pltpu.VMEM((lines, depth), jnp.bfloat16),
            pltpu.VMEM((lines, (blocks + 2) * span), jnp.float32),
            pltpu.VMEM((lines, (blocks + 2) * span), jnp.bfloat16),
            pltpu.VMEM((3 * LANES, span), jnp.bfloat16),
            pltpu.VMEM(((blocks + 2) * span, depth), jnp.bfloat16),
            pltpu.VMEM((packets, 8, depth // 2 + LANES), jnp.float32),
            pltpu.VMEM((9, n_gz, 8, depth // 2 + LANES), jnp.float32),
            pltpu.SemaphoreType.DMA((n,)),
            pltpu.SemaphoreType.DMA((n,)),
            pltpu.SemaphoreType.DMA((2, n)),
            pltpu.SemaphoreType.DMA((2, n)),
            pltpu.SemaphoreType.DMA((packets,)),
            pltpu.SemaphoreType.DMA((9, n_gz)),
        ],
        compiler_params=pltpu.CompilerParams(collective_id=0, has_side_effects=True),
    )(view_shifts, psf_width, background, camera_tiles, slot_lines)
    return pl.pallas_call(
        hand_on,
        out_shape=tuple(jax.ShapeDtypeStruct(r.shape, r.dtype) for r in results),
        in_specs=[vmem, vmem],
        out_specs=(hbm, hbm),
        scratch_shapes=[pltpu.SemaphoreType.DMA((2,))],
        compiler_params=pltpu.CompilerParams(has_side_effects=True),
    )(*[pltpu.with_memory_space_constraint(r, pltpu.VMEM) for r in results])


def solution(mesh):
    sizes = (mesh.shape["gx"], mesh.shape["gy"], mesh.shape["gz"])
    in_specs = (P(None, ("gx", "gy"), "gz"), P(None, ("gx", "gy")), P(), P(), P())
    out_specs = (P("gx", "gy", "gz"), P("gx", ("gy", "gz"), None))
    return jax.shard_map(
        functools.partial(on_device, *sizes), mesh=mesh, in_specs=in_specs, out_specs=out_specs,
        check_vma=False,
    )
```

time: 20.5 us -> 19.4 us (0.946)
  Pallas kernels: 19.7 us -> 18.6 us
    pallas_call x1, Pallas kernels: 19.1 us -> 18 us  [on_device(): pl.pallas_call(functools.partial(kernel, n_gx, n_gy, n_gz), out_shape=(pl...]
where the time goes in v1:
time: 19.4 us; the launch traced here: 19.3 us
  Pallas kernels  18.6 us (96%)
  between operations  0.64 us (3%)
    pallas_call x1, Pallas kernels, on_device(): pl.pallas_call(functools.partial(kernel, n_gx, n_gy, n_gz), out_shape=(pl...  18 us
    pallas_call x1, Pallas kernels, on_device(): pl.pallas_call(hand_on, out_shape=tuple((jax.ShapeDtypeStruct(r.shape, r....  0.68 us

profile of v1, /device:TPU:0, one launch (start us, length us, event | category | flops | bytes accessed | tf_op | source)
XLA Modules:
  0.0 19.3 jit_solution(17152270054614669874)
XLA Ops:
  0.6 18.0 %shard_map.68 = (f32[8,16,256]{2,1,0:T(8,128)S(1)}, f32[4,2,512]{2,1,0:T(2,128)S(1)}) custom-call(s32[6]{0:T(128)} %shifts_in.1, f32[6]{0:T(128)} %widths_in.1, f32[6]{0:T(128)} %backs_in.1, bf16[6,32,256]{2,1,0:T(8,128)(2,1)} %tiles_in.1, s32[6,32]{1,0:T(8,128)} %lists_in.1), custom_call_target="tpu_custom_call" | custom-call | tf_op jit(solution)/shard_map/pallas_call | solution.py:428
  18.6 0.7 %shard_map.69 = (f32[8,16,256]{2,1,0:T(8,128)}, f32[4,2,512]{2,1,0:T(2,128)}) custom-call(f32[8,16,256]{2,1,0:T(8,128)S(1)} %get-tuple-element.4.joined, f32[4,2,512]{2,1,0:T(2,128)S(1)} %get-tuple-element.5.coarse), custom_call_target="tpu_custom_call" | custom-call | tf_op jit(solution)/shard_map/pallas_call | solution.py:467

commit v2 on v1

--- a/solution.py
+++ b/solution.py
@@ -42,8 +42,8 @@
 
 def kernel(
     n_gx, n_gy, n_gz, shifts_in, widths_in, backs_in, tiles_in, lists_in, joined_out, coarse_out,
-    shifts, widths, backs, tiles, lists, local_sem, thin, weights, members, send, got, halo, vd, vd_side, est_b, partial,
-    ratio, blur_w, corr_w, parts, sums, send_sem, got_sem, pass_sem, halo_sem, part_sem, sum_sem,
+    shifts, widths, backs, tiles, lists, local_sem, thin, weights, members, send, got, mid, halo, vd, vd_side, est_b, partial,
+    ratio, blur_w, corr_w, parts, sums, send_sem, got_sem, mid_sem, next_sem, pass_sem, halo_sem, part_sem, sum_sem, ready,
 ):
     views, slots, depth = tiles_in.shape
     n = n_gx * n_gy
@@ -66,6 +66,33 @@
             recv_sem=got_sem.at[src], device_id=target, device_id_type=MESH,
         )
 
+    def across_copy(src_x, dst_x, y, target):
+        return pltpu.make_async_remote_copy(
+            src_ref=send.at[dst_x * n_gy + y, :used], dst_ref=mid.at[src_x * n_gy + y, :used],
+            send_sem=send_sem.at[dst_x * n_gy + y], recv_sem=mid_sem.at[src_x * n_gy + y], device_id=target,
+            device_id_type=MESH,
+        )
+
+    def next_copy(src_x, y, target):
+        return pltpu.make_async_remote_copy(
+            src_ref=mid.at[src_x * n_gy + y, :used], dst_ref=got.at[src_x * n_gy + gy, :used],
+            send_sem=next_sem.at[src_x * n_gy + y], recv_sem=got_sem.at[src_x * n_gy + gy], device_id=target,
+            device_id_type=MESH,
+        )
+
+    def others_x(act):
+        def one(i, carry):
+            act((gx + i) % n_gx)
+            return carry
+
+        lax.fori_loop(1, n_gx, one, 0)
+
+    def at_distance(d, act):
+        for index, sign in ((0, 1), (1, -1)):
+            @pl.when(in_y(gy + sign * d))
+            def _():
+                act(index, gy + sign * d)
+
     def halo_copy(buf, src, side, target):
         first = last if side == 0 else 0
         return pltpu.make_async_remote_copy(
@@ -124,21 +151,10 @@
     def greet(target):
         pl.semaphore_signal(barrier, inc=1, device_id=target, device_id_type=MESH)
 
-    def greet_owner(i, carry):
-        greet(owner((me + n - i) % n))
-        return carry
-
-    lax.fori_loop(1, n, greet_owner, 0)
-
-    @pl.when(gz > 0)
-    def _():
-        greet((gx, gy, gz - 1))
-
-    @pl.when(gz < n_gz - 1)
-    def _():
-        greet((gx, gy, gz + 1))
-
-    part_sources(lambda c, z, source: greet(source))
+    others_x(lambda x: greet((x, gy, gz)))
+    at_distance(1, lambda index, y: greet((gx, y, gz)))
+    for r in range(1, n_gz):
+        greet((gx, gy, (gz + r) % n_gz))
 
     pairs = (
         (tiles_in, tiles), (lists_in, lists), (shifts_in, shifts), (widths_in, widths), (backs_in, backs),
@@ -188,6 +204,55 @@
                 send[first + i, b * ROWS : (b + 1) * ROWS] = body.astype(jnp.bfloat16)
     got[me, :used] = send[me, :used]
 
+    count = n_gx - 1 + n_gz - 1 + jnp.where(in_y(gy + 1), 1, 0) + jnp.where(in_y(gy - 1), 1, 0)
+    pl.semaphore_wait(barrier, count)
+
+    def send_across(y):
+        others_x(lambda x: across_copy(gx, x, y, (x, gy, gz)).start())
+
+    def send_along(y):
+        tile_copy(me, gx * n_gy + y, (gx, y, gz)).start()
+
+    for d in range(n_gy - 1, 0, -1):
+        at_distance(d, lambda index, y: send_across(y))
+    others_x(lambda x: tile_copy(me, x * n_gy + gy, (x, gy, gz)).start())
+    at_distance(1, lambda index, y: send_along(y))
+
+    def pass_on(buf, src):
+        @pl.when(gz > 0)
+        def _():
+            halo_copy(buf, src, 1, (gx, gy, gz - 1)).start()
+
+        @pl.when(gz < n_gz - 1)
+        def _():
+            halo_copy(buf, src, 0, (gx, gy, gz + 1)).start()
+
+    pass_on(send, me)
+
+    for d in range(2, n_gy):
+        for index, sign in ((0, 1), (1, -1)):
+            @pl.when(in_y(gy + sign * (d - 1)) & in_y(gy - sign))
+            def _():
+                pl.semaphore_signal(
+                    ready.at[index, d], inc=1, device_id=(gx, gy - sign, gz), device_id_type=MESH
+                )
+
+        def reach_out(index, y):
+            pl.semaphore_wait(ready.at[index, d], 1)
+            send_along(y)
+
+        at_distance(d, reach_out)
+
+    def hand_along(y):
+        def one(x):
+            across_copy(x, gx, y, (x, gy, gz)).wait_recv()
+            next_copy(x, y, (gx, y, gz)).start()
+
+        others_x(one)
+
+    for d in range(n_gy - 1, 0, -1):
+        at_distance(d, lambda index, y: hand_along(y))
+
     step = (iota((LANES, LANES), 1) - iota((LANES, LANES), 0)).astype(jnp.float32)
     reach = iota((1, LANES), 1)
     span = views * LANES
@@ -231,39 +296,19 @@
             rows.append(jnp.where(r < rows_x * rows_y, weight, 0.0))
     weights[...] = jnp.concatenate(rows, axis=0).astype(jnp.bfloat16)
 
-    count = n - 1
-    count = count + jnp.where(gz > 0, 1, 0) + jnp.where(gz < n_gz - 1, 1, 0)
-    for dx in (-1, 0, 1):
-        per = n_gz - (1 if dx == 0 else 0)
-        per = per + jnp.where(in_y(gy + 1), 1, 0) + jnp.where(in_y(gy - 1), 1, 0)
-        count = count + jnp.where(in_x(gx + dx), per, 0)
-    pl.semaphore_wait(barrier, count)
-
-    def send_tile(i, carry):
-        o = (me + i) % n
-        tile_copy(me, o, owner(o)).start()
-        return carry
-
-    lax.fori_loop(1, n, send_tile, 0)
-
-    def pass_on(buf, src):
-        @pl.when(gz > 0)
-        def _():
-            halo_copy(buf, src, 1, (gx, gy, gz - 1)).start()
-
-        @pl.when(gz < n_gz - 1)
-        def _():
-            halo_copy(buf, src, 0, (gx, gy, gz + 1)).start()
-
-    pass_on(send, me)
-
-    def take_tile(i, carry):
-        src = (me + n - i) % n
-        tile_copy(src, me, owner(src)).wait_recv()
+    def take_tile(x, y):
+        src = x * n_gy + y
+        tile_copy(src, me, (x, y, gz)).wait_recv()
         pass_on(got, src)
-        return carry
-
-    lax.fori_loop(1, n, take_tile, 0)
+
+    others_x(lambda x: take_tile(x, gy))
+
+    def take_column(y):
+        take_tile(gx, y)
+        others_x(lambda x: take_tile(x, y))
+
+    for d in range(1, n_gy):
+        at_distance(d, lambda index, y: take_column(y))
 
     total = None
     for b in range(blocks if used == blocks * ROWS else 1):
@@ -372,6 +417,8 @@
         return carry
 
     lax.fori_loop(1, n, sent_tile, 0)
+    for d in range(1, n_gy):
+        at_distance(d, lambda index, y: others_x(lambda x: next_copy(x, y, (gx, y, gz)).wait_send()))
 
     @pl.when(gz > 0)
     def _():
@@ -445,6 +492,7 @@
             pltpu.VMEM((-(-n // 8), (views + 1) * lines, min(n, 8) * ROWS), jnp.bfloat16),
             pltpu.VMEM((n, blocks * ROWS, LANES), jnp.bfloat16),
             pltpu.VMEM((n, blocks * ROWS, LANES), jnp.bfloat16),
+            pltpu.VMEM((n, blocks * ROWS, LANES), jnp.bfloat16),
             pltpu.VMEM((2, n, ROWS, LANES), jnp.bfloat16),
             pltpu.VMEM((views * lines, depth), jnp.float32),
             pltpu.VMEM((views * lines, 2 * LANES), jnp.float32),
@@ -457,10 +505,13 @@
             pltpu.VMEM((9, n_gz, 8, depth // 2 + LANES), jnp.float32),
             pltpu.SemaphoreType.DMA((n,)),
             pltpu.SemaphoreType.DMA((n,)),
+            pltpu.SemaphoreType.DMA((n,)),
+            pltpu.SemaphoreType.DMA((n,)),
             pltpu.SemaphoreType.DMA((2, n)),
             pltpu.SemaphoreType.DMA((2, n)),
             pltpu.SemaphoreType.DMA((packets,)),
             pltpu.SemaphoreType.DMA((9, n_gz)),
+            pltpu.SemaphoreType.REGULAR((2, n_gy)),
         ],
         compiler_params=pltpu.CompilerParams(collective_id=0, has_side_effects=True),
     )(view_shifts, psf_width, background, camera_tiles, slot_lines)

time: 19.4 us -> 20.3 us (1.046)
  Pallas kernels: 18.6 us -> 19.6 us
    pallas_call x1, Pallas kernels: 18 us -> 18.9 us  [on_device(): pl.pallas_call(functools.partial(kernel, n_gx, n_gy, n_gz), out_shape=(pl...]
where the time goes in v2:
time: 20.3 us; the launch traced here: 20.2 us
  Pallas kernels  19.6 us (97%)
  between operations  0.64 us (3%)
    pallas_call x1, Pallas kernels, on_device(): pl.pallas_call(functools.partial(kernel, n_gx, n_gy, n_gz), out_shape=(pl...  18.9 us
    pallas_call x1, Pallas kernels, on_device(): pl.pallas_call(hand_on, out_shape=tuple((jax.ShapeDtypeStruct(r.shape, r....  0.68 us

profile of v2, /device:TPU:0, one launch (start us, length us, event | category | flops | bytes accessed | tf_op | source)
XLA Modules:
  0.0 20.2 jit_solution(10085793202014987103)
XLA Ops:
  0.6 18.9 %shard_map.68 = (f32[8,16,256]{2,1,0:T(8,128)S(1)}, f32[4,2,512]{2,1,0:T(2,128)S(1)}) custom-call(s32[6]{0:T(128)} %shifts_in.1, f32[6]{0:T(128)} %widths_in.1, f32[6]{0:T(128)} %backs_in.1, bf16[6,32,256]{2,1,0:T(8,128)(2,1)} %tiles_in.1, s32[6,32]{1,0:T(8,128)} %lists_in.1), custom_call_target="tpu_custom_call" | custom-call | tf_op jit(solution)/shard_map/pallas_call | solution.py:475
  19.5 0.7 %shard_map.69 = (f32[8,16,256]{2,1,0:T(8,128)}, f32[4,2,512]{2,1,0:T(2,128)}) custom-call(f32[8,16,256]{2,1,0:T(8,128)S(1)} %get-tuple-element.4.joined, f32[4,2,512]{2,1,0:T(2,128)S(1)} %get-tuple-element.5.coarse), custom_call_target="tpu_custom_call" | custom-call | tf_op jit(solution)/shard_map/pallas_call | solution.py:518

commit v3 on v1

--- a/solution.py
+++ b/solution.py
@@ -43,7 +43,7 @@
 def kernel(
     n_gx, n_gy, n_gz, shifts_in, widths_in, backs_in, tiles_in, lists_in, joined_out, coarse_out,
     shifts, widths, backs, tiles, lists, local_sem, thin, weights, members, send, got, halo, vd, vd_side, est_b, partial,
-    ratio, blur_w, corr_w, parts, sums, send_sem, got_sem, pass_sem, halo_sem, part_sem, sum_sem,
+    ratio, blur_w, corr_w, parts, edges, sums, edge_sums, send_sem, got_sem, pass_sem, halo_sem, part_sem, sum_sem,
 ):
     views, slots, depth = tiles_in.shape
     n = n_gx * n_gy
@@ -73,10 +73,14 @@
             send_sem=pass_sem.at[side, src], recv_sem=halo_sem.at[side, src], device_id=target, device_id_type=MESH,
         )
 
-    def part_copy(p, c, src_z, target):
+    def part_copy(dxi, part, cy, src_z, target):
+        if dxi == 1:
+            src, dst = parts.at[part], sums.at[cy, src_z]
+        else:
+            src, dst = edges.at[dxi // 2, part], edge_sums.at[dxi // 2, cy, src_z]
         return pltpu.make_async_remote_copy(
-            src_ref=parts.at[p], dst_ref=sums.at[c, src_z], send_sem=part_sem.at[p],
-            recv_sem=sum_sem.at[c, src_z], device_id=target, device_id_type=MESH,
+            src_ref=src, dst_ref=dst, send_sem=part_sem.at[dxi * group + part],
+            recv_sem=sum_sem.at[dxi * 3 + cy, src_z], device_id=target, device_id_type=MESH,
         )
 
     def in_x(x):
@@ -91,15 +95,15 @@
             def _():
                 @pl.when(in_y(gy + 1))
                 def _():
-                    act(dxi * group + n_gz, dxi * 3 + 2, (gx + dx, gy + 1, 0))
+                    act(dxi, n_gz, 2, (gx + dx, gy + 1, 0))
 
                 @pl.when(in_y(gy - 1))
                 def _():
-                    act(dxi * group + n_gz + 1, dxi * 3, (gx + dx, gy - 1, n_gz - 1))
+                    act(dxi, n_gz + 1, 0, (gx + dx, gy - 1, n_gz - 1))
 
                 for r in range(1 if dx == 0 else 0, n_gz):
                     k = (gz + r) % n_gz
-                    act(dxi * group + k, dxi * 3 + 1, (gx + dx, gy, k))
+                    act(dxi, k, 1, (gx + dx, gy, k))
 
     def part_sources(act):
         for dxi, dx in enumerate((-1, 0, 1)):
@@ -107,17 +111,17 @@
             def _():
                 for r in range(1 if dx == 0 else 0, n_gz):
                     z = (gz + r) % n_gz
-                    act(dxi * 3 + 1, z, (gx - dx, gy, z))
+                    act(dxi, 1, z, (gx - dx, gy, z))
 
                 @pl.when(in_y(gy - 1) & (gz == 0))
                 def _():
                     for z in range(n_gz):
-                        act(dxi * 3 + 2, z, (gx - dx, gy - 1, z))
+                        act(dxi, 2, z, (gx - dx, gy - 1, z))
 
                 @pl.when(in_y(gy + 1) & (gz == n_gz - 1))
                 def _():
                     for z in range(n_gz):
-                        act(dxi * 3, z, (gx - dx, gy + 1, z))
+                        act(dxi, 0, z, (gx - dx, gy + 1, z))
 
     barrier = pltpu.get_barrier_semaphore()
 
@@ -138,7 +142,7 @@
     def _():
         greet((gx, gy, gz + 1))
 
-    part_sources(lambda c, z, source: greet(source))
+    part_sources(lambda dxi, cy, z, source: greet(source))
 
     pairs = (
         (tiles_in, tiles), (lists_in, lists), (shifts_in, shifts), (widths_in, widths), (backs_in, backs),
@@ -188,6 +192,32 @@
                 send[first + i, b * ROWS : (b + 1) * ROWS] = body.astype(jnp.bfloat16)
     got[me, :used] = send[me, :used]
 
+    count = n - 1
+    count = count + jnp.where(gz > 0, 1, 0) + jnp.where(gz < n_gz - 1, 1, 0)
+    for dx in (-1, 0, 1):
+        per = n_gz - (1 if dx == 0 else 0)
+        per = per + jnp.where(in_y(gy + 1), 1, 0) + jnp.where(in_y(gy - 1), 1, 0)
+        count = count + jnp.where(in_x(gx + dx), per, 0)
+    pl.semaphore_wait(barrier, count)
+
+    def send_tile(i, carry):
+        o = (me + i) % n
+        tile_copy(me, o, owner(o)).start()
+        return carry
+
+    lax.fori_loop(1, n, send_tile, 0)
+
+    def pass_on(buf, src):
+        @pl.when(gz > 0)
+        def _():
+            halo_copy(buf, src, 1, (gx, gy, gz - 1)).start()
+
+        @pl.when(gz < n_gz - 1)
+        def _():
+            halo_copy(buf, src, 0, (gx, gy, gz + 1)).start()
+
+    pass_on(send, me)
+
     step = (iota((LANES, LANES), 1) - iota((LANES, LANES), 0)).astype(jnp.float32)
     reach = iota((1, LANES), 1)
     span = views * LANES
@@ -221,41 +251,26 @@
     thin[...] = tap(z - 2 * k + 1).astype(jnp.bfloat16)
     r = iota((8, lines), 0)
     column = iota((8, lines), 1)
-    rows = []
-    for dx in (-1, 0, 1):
-        for t in range(group):
-            dy, z_part = (0, t) if t < n_gz else ((1, 0) if t == n_gz else (-1, n_gz - 1))
-            i = rows_x * dx + r // rows_y
-            j = (CY // 2) * dy + rows_y * z_part + r % rows_y
-            weight = tap(column // CY - 2 * i + 1) * tap(column % CY - 2 * j + 1)
-            rows.append(jnp.where(r < rows_x * rows_y, weight, 0.0))
+
+    def weight_of(dx, t, i, j):
+        dy, z_part = (0, t) if t < n_gz else ((1, 0) if t == n_gz else (-1, n_gz - 1))
+        i = rows_x * dx + i
+        j = (CY // 2) * dy + rows_y * z_part + j
+        return tap(column // CY - 2 * i + 1) * tap(column % CY - 2 * j + 1)
+
+    rows = [
+        jnp.where(r < rows_x * rows_y, weight_of(0, t, r // rows_y, r % rows_y), 0.0) for t in range(group)
+    ]
+    for first in range(0, 2 * group * rows_y, 8):
+        block = jnp.zeros((8, lines), jnp.float32)
+        for e in range(2 * group):
+            for j in range(rows_y):
+                at = e * rows_y + j - first
+                if 0 <= at < 8:
+                    dx, i = (-1, rows_x - 1) if e < group else (1, 0)
+                    block = jnp.where(r == at, weight_of(dx, e % group, i, j), block)
+        rows.append(block)
     weights[...] = jnp.concatenate(rows, axis=0).astype(jnp.bfloat16)
-
-    count = n - 1
-    count = count + jnp.where(gz > 0, 1, 0) + jnp.where(gz < n_gz - 1, 1, 0)
-    for dx in (-1, 0, 1):
-        per = n_gz - (1 if dx == 0 else 0)
-        per = per + jnp.where(in_y(gy + 1), 1, 0) + jnp.where(in_y(gy - 1), 1, 0)
-        count = count + jnp.where(in_x(gx + dx), per, 0)
-    pl.semaphore_wait(barrier, count)
-
-    def send_tile(i, carry):
-        o = (me + i) % n
-        tile_copy(me, o, owner(o)).start()
-        return carry
-
-    lax.fori_loop(1, n, send_tile, 0)
-
-    def pass_on(buf, src):
-        @pl.when(gz > 0)
-        def _():
-            halo_copy(buf, src, 1, (gx, gy, gz - 1)).start()
-
-        @pl.when(gz < n_gz - 1)
-        def _():
-            halo_copy(buf, src, 0, (gx, gy, gz + 1)).start()
-
-    pass_on(send, me)
 
     def take_tile(i, carry):
         src = (me + n - i) % n
@@ -363,9 +378,12 @@
     high = halved.astype(jnp.bfloat16)
     low = (halved - high.astype(jnp.float32)).astype(jnp.bfloat16)
     shares = (dot(weights[...], high) + dot(weights[...], low)) * (1.0 / 64)
-    parts[...] = shares.reshape(3 * group, 8, half_depth + LANES)
-    part_sends(lambda p, c, target: part_copy(p, c, gz, target).start())
-    sums[4, gz] = parts[group + gz]
+    parts[...] = shares[: group * 8].reshape(group, 8, half_depth + LANES)
+    for e in range(2 * group):
+        at = group * 8 + e * rows_y
+        edges[e // group, e % group] = shares[at : at + rows_y]
+    part_sends(lambda dxi, part, cy, target: part_copy(dxi, part, cy, gz, target).start())
+    sums[1, gz] = parts[gz]
     def sent_tile(i, carry):
         o = (me + i) % n
         tile_copy(me, o, owner(o)).wait_send()
@@ -383,15 +401,21 @@
         for src in range(n):
             halo_copy(got, src, 0, (gx, gy, gz)).wait_send()
 
-    part_sources(lambda c, s, source: part_copy(0, c, s, source).wait_recv())
+    part_sources(lambda dxi, cy, s, source: part_copy(dxi, 0, cy, s, source).wait_recv())
     totals = []
     for s in range(n_gz):
-        total = sums[4, s]
-        for dxi, dx in enumerate((-1, 0, 1)):
-            for c, there in ((0, in_y(gy + 1) & (gz == n_gz - 1)), (1, gz >= 0), (2, in_y(gy - 1) & (gz == 0))):
-                if dx == 0 and c == 1:
-                    continue
-                total = total + jnp.where(in_x(gx - dx) & there, sums[dxi * 3 + c, s], 0.0)
+        total = sums[1, s]
+        above, below = in_y(gy + 1) & (gz == n_gz - 1), in_y(gy - 1) & (gz == 0)
+        total = total + jnp.where(above, sums[0, s], 0.0) + jnp.where(below, sums[2, s], 0.0)
+        sides = []
+        for index, dx in ((1, 1), (0, -1)):
+            side = edge_sums[index, 1, s]
+            side = side + jnp.where(above, edge_sums[index, 0, s], 0.0) + jnp.where(below, edge_sums[index, 2, s], 0.0)
+            sides.append(jnp.where(in_x(gx - dx), side, 0.0))
+        sides.insert(1, jnp.zeros(((rows_x - 2) * rows_y, half_depth + LANES), jnp.float32))
+        if rows_x * rows_y < 8:
+            sides.append(jnp.zeros((8 - rows_x * rows_y, half_depth + LANES), jnp.float32))
+        total = total + jnp.concatenate(sides, axis=0)
         totals.append(total)
     lane = iota((8, half_depth), 1)
     for s in range(n_gz):
@@ -404,7 +428,7 @@
             total = total + jnp.where(lane == half_depth - 1, spread_lanes(before, half_depth), 0.0)
         for i in range(rows_x):
             coarse_out[i, :, s * half_depth : (s + 1) * half_depth] = total[i * rows_y : (i + 1) * rows_y]
-    part_sends(lambda p, c, target: part_copy(p, c, gz, target).wait_send())
+    part_sends(lambda dxi, part, cy, target: part_copy(dxi, part, cy, gz, target).wait_send())
 
 
 def hand_on(joined, coarse, joined_out, coarse_out, sem):
@@ -419,7 +443,9 @@
 def on_device(n_gx, n_gy, n_gz, camera_tiles, slot_lines, view_shifts, psf_width, background):
     views, slots, depth = camera_tiles.shape
     n = n_gx * n_gy
-    packets = 3 * (n_gz + 2)
+    group = n_gz + 2
+    packets = 3 * group
+    rows_y = CY // 2 // n_gz
     blocks = depth // LANES
     lines = CX * CY
     span = views * LANES
@@ -441,7 +467,7 @@
             pltpu.VMEM((views, slots), jnp.int32),
             pltpu.SemaphoreType.DMA((5,)),
             pltpu.VMEM((depth, depth // 2 + LANES), jnp.bfloat16),
-            pltpu.VMEM((packets * 8, lines), jnp.bfloat16),
+            pltpu.VMEM((group * 8 + -(-2 * group * rows_y // 8) * 8, lines), jnp.bfloat16),
             pltpu.VMEM((-(-n // 8), (views + 1) * lines, min(n, 8) * ROWS), jnp.bfloat16),
             pltpu.VMEM((n, blocks * ROWS, LANES), jnp.bfloat16),
             pltpu.VMEM((n, blocks * ROWS, LANES), jnp.bfloat16),
@@ -453,8 +479,10 @@
             pltpu.VMEM((lines, (blocks + 2) * span), jnp.bfloat16),
             pltpu.VMEM((3 * LANES, span), jnp.bfloat16),
             pltpu.VMEM(((blocks + 2) * span, depth), jnp.bfloat16),
-            pltpu.VMEM((packets, 8, depth // 2 + LANES), jnp.float32),
-            pltpu.VMEM((9, n_gz, 8, depth // 2 + LANES), jnp.float32),
+            pltpu.VMEM((group, 8, depth // 2 + LANES), jnp.float32),
+            pltpu.VMEM((2, group, rows_y, depth // 2 + LANES), jnp.float32),
+            pltpu.VMEM((3, n_gz, 8, depth // 2 + LANES), jnp.float32),
+            pltpu.VMEM((2, 3, n_gz, rows_y, depth // 2 + LANES), jnp.float32),
             pltpu.SemaphoreType.DMA((n,)),
             pltpu.SemaphoreType.DMA((n,)),
             pltpu.SemaphoreType.DMA((2, n)),

time: 19.4 us -> 18.7 us (0.964)
  Pallas kernels: 18.6 us -> 17.9 us
    pallas_call x1, Pallas kernels: 18 us -> 17.3 us  [on_device(): pl.pallas_call(functools.partial(kernel, n_gx, n_gy, n_gz), out_shape=(pl...]
where the time goes in v3:
time: 18.7 us; the launch traced here: 18.6 us
  Pallas kernels  17.9 us (96%)
  between operations  0.64 us (3%)
    pallas_call x1, Pallas kernels, on_device(): pl.pallas_call(functools.partial(kernel, n_gx, n_gy, n_gz), out_shape=(pl...  17.3 us
    pallas_call x1, Pallas kernels, on_device(): pl.pallas_call(hand_on, out_shape=tuple((jax.ShapeDtypeStruct(r.shape, r....  0.68 us

profile of v3, /device:TPU:0, one launch (start us, length us, event | category | flops | bytes accessed | tf_op | source)
XLA Modules:
  0.0 18.6 jit_solution(9231567748704072034)
XLA Ops:
  0.6 17.3 %shard_map.68 = (f32[8,16,256]{2,1,0:T(8,128)S(1)}, f32[4,2,512]{2,1,0:T(2,128)S(1)}) custom-call(s32[6]{0:T(128)} %shifts_in.1, f32[6]{0:T(128)} %widths_in.1, f32[6]{0:T(128)} %backs_in.1, bf16[6,32,256]{2,1,0:T(8,128)(2,1)} %tiles_in.1, s32[6,32]{1,0:T(8,128)} %lists_in.1), custom_call_target="tpu_custom_call" | custom-call | tf_op jit(solution)/shard_map/pallas_call | solution.py:454
  17.9 0.7 %shard_map.69 = (f32[8,16,256]{2,1,0:T(8,128)}, f32[4,2,512]{2,1,0:T(2,128)}) custom-call(f32[8,16,256]{2,1,0:T(8,128)S(1)} %get-tuple-element.4.joined, f32[4,2,512]{2,1,0:T(2,128)S(1)} %get-tuple-element.5.coarse), custom_call_target="tpu_custom_call" | custom-call | tf_op jit(solution)/shard_map/pallas_call | solution.py:495
